TPU v7x, 32 devices: a whole 2x2x4 slice. The times are simulated.
32 devices in a mesh: seq: 8 (over z, x), head: 4 (over y, core).
Axes of the slice: x: 2, y: 2, z: 4, core: 2. Of those that a mesh axis runs over, the one named last changes fastest.
Arguments:
- queries: bfloat16 [9216, 32, 128], P(('seq', 'head')), may hold values from -4 to 4
- key_states: bfloat16 [9216, 4, 128], P(('seq', 'head')), may hold values from -4 to 4
- value_states: bfloat16 [9216, 4, 128], P(('seq', 'head')), may hold values from -6 to 6
- outputs: bfloat16 [9216, 32, 128], P(('seq', 'head')), may hold values from -6 to 6
- output_grad: bfloat16 [9216, 32, 128], P(('seq', 'head')), may hold values from -96 to 96
- logsumexp: float32 [9216, 32], P(('seq', 'head')), may hold values from 6.8 to 7.8
- random_owner: int32 [72, 3], replicated, may hold values from 0 to 7, all different within a row; in each aligned block of 9 rows (0 to 8, 9 to 17, ...) at most 4 rows name the same one
- random_slot: int32 [72, 3], replicated, may hold values from 0 to 8
Outputs:
- query_grad: bfloat16 [9216, 32, 128], P(('seq', 'head'))
- key_grad: bfloat16 [9216, 4, 128], P(('seq', 'head'))
- value_grad: bfloat16 [9216, 4, 128], P(('seq', 'head'))
Inputs may be any that keep to these rules, and one draw needn't show every extreme that they name: `random_owner`: each row names 3 different indices. Within the 9 rows of one index of seq (aligned blocks of 9 rows), no index of seq appears more than 4 times, and some index appears exactly 4 times in some block.
All inputs are finite; a program needn't handle non-finite values.
Results may differ from a plain program's by a relative error of at most 0.005.
Values may be sent and summed in bfloat16 or wider, within the bound.
A program may use at most 128 MiB of HBM per device.

v0:
```python
import functools
import math

import jax
import jax.numpy as jnp
from jax import lax
from jax.experimental import pallas as pl
from jax.experimental.pallas import tpu as pltpu
from jax.sharding import PartitionSpec as P

HD = 128
BLK = 128
G = 2
RND = 3
MESH = pl.DeviceIdType.MESH
F32 = jnp.float32
BF16 = jnp.bfloat16
LOG2E = math.log2(math.e)


def greet(n_seq, n_head, seq, head):
    barrier = pltpu.get_barrier_semaphore()

    def to_head(d, c):
        pl.semaphore_signal(
            barrier, inc=1, device_id={"head": lax.rem(head + d, n_head)}, device_id_type=MESH
        )
        return c

    def to_seq(d, c):
        pl.semaphore_signal(
            barrier, inc=1, device_id={"seq": lax.rem(seq + d, n_seq)}, device_id_type=MESH
        )
        return c

    lax.fori_loop(1, n_head, to_head, 0)
    lax.fori_loop(1, n_seq, to_seq, 0)
    pl.semaphore_wait(barrier, n_head + n_seq - 2)


def remote(src, dst, send, recv, **where):
    return pltpu.make_async_remote_copy(
        src_ref=src,
        dst_ref=dst,
        send_sem=send,
        recv_sem=recv,
        device_id=where,
        device_id_type=MESH,
    )


def dot(a, b, ca, cb):
    return lax.dot_general(a, b, (((ca,), (cb,)), ((), ())), preferred_element_type=F32)


def pair_grads(k, v, shifts, q, g, delta, scaling):
    scores = dot(k, q, 1, 1) * (scaling * LOG2E)
    weights = jnp.concatenate(
        [jnp.exp2(scores[i * BLK : (i + 1) * BLK] - shift) for i, shift in enumerate(shifts)],
        axis=0,
    )
    score_grad = (weights * (dot(v, g, 1, 1) - delta)).astype(BF16)
    dv = dot(weights.astype(BF16), g, 1, 0)
    dk = dot(score_grad, q, 1, 0) * scaling
    return dk, dv, dot(k, score_grad, 0, 0)


def fused(
    n_seq, n_head, most, blocks,
    pick, pos, back, bias, share, q_in, g_in, kv_in, ld_in,
    dq_out, kv_out,
    q_all, g_all, ld_all, kv_ext, glob, rand, picked, held, acc, gacc, dq_acc, dq_all,
    rpart, rback, halo_part, halo, gpart, gall, kv_sum,
    hs, hr, ls, ss, sr, ns, nr, gs, gr, rs, rr,
):
    seq, head = lax.axis_index("seq"), lax.axis_index("head")
    toks = kv_in.shape[2]
    group = q_in.shape[1] // n_head
    rows = toks * group
    span = n_head * toks
    lines = rows // 128
    step = rows * n_head // blocks
    scaling = 1.0 / HD**0.5
    greet(n_seq, n_head, seq, head)

    def partner(d):
        base = lax.rem(head + 2 * (d // 2), n_head)
        return base + (1 - 2 * lax.rem(base, 2)) if d % 2 else base

    here = pl.ds(pl.multiple_of(head * toks, toks), toks)
    q_to = q_all.at[here]
    g_to = g_all.at[here]
    kv_to = kv_ext.at[:, pl.ds(pl.multiple_of(BLK + head * toks, 32), toks), :]
    ld_to = ld_all.at[:, pl.ds(head * lines, lines)]

    def heads_of(ref, peer):
        return ref.at[:, pl.ds(pl.multiple_of(peer * group, group), group), :]

    def head_copy(kind, d):
        peer = partner(d)
        src, dst = (
            (kv_in.at[peer], kv_to),
            (ld_in.at[peer], ld_to),
            (heads_of(q_in, peer), q_to),
            (heads_of(g_in, peer), g_to),
        )[kind]
        return remote(src, dst, hs.at[kind, d], hr.at[kind, d], head=peer)

    own = [
        pltpu.make_async_copy(kv_in.at[head], kv_to, ls.at[0]),
        pltpu.make_async_copy(ld_in.at[head], ld_to, ls.at[1]),
        pltpu.make_async_copy(heads_of(q_in, head), q_to, ls.at[2]),
        pltpu.make_async_copy(heads_of(g_in, head), g_to, ls.at[3]),
    ]
    for kind in range(4):
        own[kind].start()
    for kind in range(4):
        for d in list(range(2, n_head)) + [1]:
            head_copy(kind, d).start()
    own[0].wait()
    for d in range(1, n_head):
        head_copy(0, d).wait_recv()

    up, down = lax.rem(seq + 1, n_seq), lax.rem(seq + n_seq - 1, n_seq)
    to_up = remote(
        kv_ext.at[:, pl.ds(span, BLK), :], kv_ext.at[:, pl.ds(0, BLK), :],
        ns.at[0], nr.at[0], seq=up,
    )
    to_down = remote(
        kv_ext.at[:, pl.ds(BLK, BLK), :], kv_ext.at[:, pl.ds(BLK + span, BLK), :],
        ns.at[1], nr.at[1], seq=down,
    )

    def rand_copy(d):
        peer = lax.rem(seq + d, n_seq)
        return remote(
            picked.at[pl.ds(peer * most, most)], rand.at[pl.ds(seq * most, most)],
            ss.at[d], sr.at[d], seq=peer,
        )

    def glob_copy(d):
        return remote(kv_ext.at[:, pl.ds(BLK, G * BLK), :], glob, gs.at[d], gr.at[0], seq=d)

    def loop(low, high, body):
        def run(i, c):
            body(i)
            return c

        lax.fori_loop(low, high, run, 0)

    def fill(i):
        picked[i] = held[pick[i]]

    for block in range(blocks):
        held[block] = kv_ext[:, (block + 1) * BLK : (block + 2) * BLK, :]
    loop(0, n_seq * most, fill)
    to_up.start()
    to_down.start()

    @pl.when(seq == 0)
    def _():
        loop(1, n_seq, lambda d: glob_copy(d).start())
        glob[...] = kv_ext[:, BLK : BLK + G * BLK, :]

    loop(1, n_seq, lambda d: rand_copy(d).start())
    rand[pl.ds(seq * most, most)] = picked[pl.ds(seq * most, most)]

    acc[...] = jnp.zeros_like(acc)
    gacc[...] = jnp.zeros_like(gacc)
    to_up.wait()
    to_down.wait()

    @pl.when(seq > 0)
    def _():
        glob_copy(0).wait_recv()

    for kind in range(1, 4):
        own[kind].wait()
        head_copy(kind, 1).wait_recv()
    for d in range(2, n_head):
        head_copy(1, d).wait_recv()

    turn = head // (n_head // 2)

    def order(i):
        return i + turn * (blocks - 1 - 2 * i)

    def operands(b):
        spot = pl.ds(pl.multiple_of(b * BLK, BLK), BLK)
        per = step // 128

        def lanes(part):
            tile = ld_all[part, pl.ds(b * per, per)]
            return jnp.concatenate([tile[r] for r in range(per)], axis=1)

        flat = (step, HD)
        return q_all[spot].reshape(flat), g_all[spot].reshape(flat), lanes(0) * LOG2E, lanes(1)

    def near(i, fresh):
        b = order(i)
        q, g, lse, delta = operands(b)
        at = pl.multiple_of(b * BLK, BLK)
        win = pl.ds(at, 3 * BLK)
        dk, dv, dq = pair_grads(glob[0], glob[1], [lse] * G, q, g, delta, scaling)
        gacc[0] += dk
        gacc[1] += dv
        shifts = [lse + bias[b * (3 + RND) + j] for j in range(3)]
        dk, dv, more = pair_grads(kv_ext[0, win, :], kv_ext[1, win, :], shifts, q, g, delta, scaling)
        acc[0, win, :] += dk
        acc[1, win, :] += dv
        if fresh:
            dq_acc[b] = dq + more
        else:
            total = dq_acc[b] + dq + more
            dq_all[pl.ds(at, BLK)] = (total.T * scaling).astype(BF16).reshape(BLK, group, HD)

    def far(i, fresh):
        b = order(i)
        q, g, lse, delta = operands(b)
        at = pl.multiple_of(b * BLK, BLK)
        found = [rand[pos[b * RND + j]] for j in range(RND)]
        k = jnp.concatenate([f[0] for f in found], axis=0)
        v = jnp.concatenate([f[1] for f in found], axis=0)
        shifts = [lse + bias[b * (3 + RND) + 3 + j] for j in range(RND)]
        dk, dv, dq = pair_grads(k, v, shifts, q, g, delta, scaling)
        for j in range(RND):
            rpart[b * RND + j, 0] = dk[j * BLK : (j + 1) * BLK].astype(BF16)
            rpart[b * RND + j, 1] = dv[j * BLK : (j + 1) * BLK].astype(BF16)
        if fresh:
            dq_acc[b] = dq
        else:
            total = dq_acc[b] + dq
            dq_all[pl.ds(at, BLK)] = (total.T * scaling).astype(BF16).reshape(BLK, group, HD)

    early = span // 2 // BLK
    loop(0, early, lambda i: near(i, True))
    loop(1, n_seq, lambda d: rand_copy(d).wait())
    loop(0, early, lambda i: far(i, False))
    for kind in range(2, 4):
        for d in range(2, n_head):
            head_copy(kind, d).wait_recv()
    loop(early, blocks, lambda i: far(i, True))

    def gather(i):
        picked[i] = rpart[back[i]]

    def back_copy(d):
        peer = lax.rem(seq + d, n_seq)
        return remote(
            picked.at[pl.ds(peer * most, most)], rback.at[pl.ds(seq * most, most)],
            rs.at[d], rr.at[d], seq=peer,
        )

    loop(0, n_seq * most, gather)
    rback[pl.ds(seq * most, most)] = picked[pl.ds(seq * most, most)]
    loop(1, n_seq, lambda d: back_copy(d).start())
    loop(early, blocks, lambda i: near(i, False))

    halo_part[0] = acc[:, 0:BLK, :].astype(BF16)
    halo_part[1] = acc[:, BLK + span :, :].astype(BF16)
    gpart[...] = gacc[...].astype(BF16)

    def dq_copy(d):
        peer = partner(d)
        src = dq_all.at[pl.ds(pl.multiple_of(peer * toks, toks), toks)]
        return remote(src, heads_of(dq_out, head), hs.at[4, d], hr.at[4, d], head=peer)

    def kv_copy(d):
        peer = partner(d)
        src = kv_sum.at[:, pl.ds(pl.multiple_of(peer * toks, 32), toks), :]
        return remote(src, kv_out.at[head], hs.at[5, d], hr.at[5, d], head=peer)

    def part_copy():
        return remote(gpart, gall.at[seq], gs.at[0], gr.at[seq], seq=0)

    down_grad = remote(halo_part.at[0], halo.at[0], ns.at[2], nr.at[2], seq=down)
    up_grad = remote(halo_part.at[1], halo.at[1], ns.at[3], nr.at[3], seq=up)
    own_dq = pltpu.make_async_copy(dq_all.at[here], heads_of(dq_out, head), ls.at[4])
    for d in list(range(2, n_head)) + [1]:
        dq_copy(d).start()
    own_dq.start()
    down_grad.start()
    up_grad.start()

    @pl.when(seq > 0)
    def _():
        part_copy().start()

    for kind in range(4):
        for d in range(1, n_head):
            head_copy(kind, d).wait_send()

    @pl.when(seq == 0)
    def _():
        loop(1, n_seq, lambda d: glob_copy(d).wait_send())
        gall[0] = gpart[...]

        def arrive(d):
            remote(gpart, gall.at[d], gs.at[0], gr.at[d], seq=0).wait_recv()

        loop(1, n_seq, arrive)

        def add(d):
            gacc[...] += gall[d].astype(F32)

        loop(1, n_seq, add)
        acc[:, BLK : BLK + G * BLK, :] += gacc[...]

    @pl.when(seq > 0)
    def _():
        part_copy().wait_send()

    down_grad.wait()
    up_grad.wait()
    acc[:, BLK : 2 * BLK, :] += halo[1].astype(F32)
    acc[:, span : span + BLK, :] += halo[0].astype(F32)
    def absorb(d):
        base = lax.rem(seq + n_seq - d, n_seq) * most

        def block_sum(block):
            over = pl.ds(pl.multiple_of(block * BLK + BLK, BLK), BLK)
            for part in range(2):
                value = acc[part, over, :]
                for m in range(most):
                    value = value + share[block, base + m] * rback[base + m, part].astype(F32)
                acc[part, over, :] = value

        loop(0, blocks, block_sum)

    def take(d):
        back_copy(d).wait()
        absorb(d)

    absorb(0)
    loop(1, n_seq, take)
    kv_sum[...] = acc[:, BLK : BLK + span, :].astype(BF16)
    own_kv = pltpu.make_async_copy(
        kv_sum.at[:, pl.ds(pl.multiple_of(head * toks, 32), toks), :], kv_out.at[head], ls.at[5]
    )
    for d in list(range(2, n_head)) + [1]:
        kv_copy(d).start()
    own_kv.start()
    own_dq.wait()
    for d in range(1, n_head):
        dq_copy(d).wait()
    own_kv.wait()
    for d in range(1, n_head):
        kv_copy(d).wait()


def per_device(
    n_seq, n_head,
    queries, key_states, value_states, outputs, output_grad, logsumexp, random_owner, random_slot,
):
    toks, heads, _ = queries.shape
    group = heads // n_head
    rows = toks * group
    span = toks * n_head
    blocks = span // BLK
    per_row = blocks * RND
    most = max(1, (per_row + n_seq - 1) // n_seq)
    seq = lax.axis_index("seq")
    vmem = pl.BlockSpec(memory_space=pltpu.VMEM)
    smem = pl.BlockSpec(memory_space=pltpu.SMEM)
    hbm = pl.BlockSpec(memory_space=pl.ANY)
    dma = pltpu.SemaphoreType.DMA

    delta = jnp.sum(output_grad.astype(F32) * outputs.astype(F32), axis=-1)

    ld = jnp.stack([logsumexp, delta]).reshape(2, toks, n_head, group)
    ld = jnp.transpose(ld, (2, 0, 1, 3)).reshape(n_head, 2, rows // 128, 1, 128)
    kv = jnp.transpose(jnp.stack([key_states, value_states]), (2, 0, 1, 3))

    owner_table = random_owner.reshape(n_seq, per_row)
    slot_table = random_slot.reshape(n_seq, per_row)
    entry = jnp.arange(per_row, dtype=jnp.int32)
    rank_table = jnp.sum(
        (
            (owner_table[:, :, None] == owner_table[:, None, :])
            & (entry[None, :] < entry[:, None])[None]
        ).astype(jnp.int32),
        axis=2,
    )
    hits = (owner_table == seq)[:, :, None] & (
        rank_table[:, :, None] == jnp.arange(most, dtype=jnp.int32)
    )
    pick = jnp.sum(jnp.where(hits, slot_table[:, :, None] + 1, 0), axis=1).reshape(-1) - 1
    share = (pick[None, :] == jnp.arange(blocks, dtype=jnp.int32)[:, None]).astype(F32)
    my_owner = lax.dynamic_slice_in_dim(owner_table, seq, 1, 0).reshape(-1)
    my_slot = lax.dynamic_slice_in_dim(slot_table, seq, 1, 0).reshape(-1)
    my_rank = lax.dynamic_slice_in_dim(rank_table, seq, 1, 0).reshape(-1)
    pos = my_owner * most + my_rank
    ids = seq * blocks + jnp.arange(blocks, dtype=jnp.int32)
    near = ids[:, None] + jnp.arange(-1, 2, dtype=jnp.int32)[None, :]
    far = (my_owner * blocks + my_slot).reshape(blocks, RND)
    okay = jnp.concatenate(
        [
            (near >= G) & (near <= n_seq * blocks - 1),
            (far >= G) & (jnp.abs(far - ids[:, None]) >= 2),
        ],
        axis=1,
    )
    bias = jnp.where(okay, 0.0, 1e30).astype(F32).reshape(-1)

    back = jnp.sum(
        jnp.where(
            pos[None, :] == jnp.arange(n_seq * most, dtype=jnp.int32)[:, None],
            jnp.arange(per_row, dtype=jnp.int32)[None, :],
            0,
        ),
        axis=1,
    )
    slots = n_seq * most
    step = BLK * group
    query_grad, kv_all = pl.pallas_call(
        functools.partial(fused, n_seq, n_head, most, blocks),
        out_shape=[
            jax.ShapeDtypeStruct((toks, heads, HD), BF16),
            jax.ShapeDtypeStruct((n_head, 2, toks, HD), BF16),
        ],
        in_specs=[smem] * 5 + [hbm, hbm, vmem, vmem],
        out_specs=[hbm, vmem],
        scratch_shapes=[
            pltpu.VMEM((span, group, HD), BF16),
            pltpu.VMEM((span, group, HD), BF16),
            pltpu.VMEM((2, n_head * rows // 128, 1, 128), F32),
            pltpu.VMEM((2, span + 2 * BLK, HD), BF16),
            pltpu.VMEM((2, G * BLK, HD), BF16),
            pltpu.VMEM((slots, 2, BLK, HD), BF16),
            pltpu.VMEM((slots, 2, BLK, HD), BF16),
            pltpu.VMEM((blocks, 2, BLK, HD), BF16),
            pltpu.VMEM((2, span + 2 * BLK, HD), F32),
            pltpu.VMEM((2, G * BLK, HD), F32),
            pltpu.VMEM((blocks, HD, step), F32),
            pltpu.VMEM((span, group, HD), BF16),
            pltpu.VMEM((per_row, 2, BLK, HD), BF16),
            pltpu.VMEM((slots, 2, BLK, HD), BF16),
            pltpu.VMEM((2, 2, BLK, HD), BF16),
            pltpu.VMEM((2, 2, BLK, HD), BF16),
            pltpu.VMEM((2, G * BLK, HD), BF16),
            pltpu.VMEM((n_seq, 2, G * BLK, HD), BF16),
            pltpu.VMEM((2, span, HD), BF16),
            dma((6, n_head)), dma((6, n_head)), dma((6,)),
            dma((n_seq,)), dma((n_seq,)), dma((4,)), dma((4,)), dma((n_seq,)), dma((n_seq,)),
            dma((n_seq,)), dma((n_seq,)),
        ],
        compiler_params=pltpu.CompilerParams(
            collective_id=0, has_side_effects=True, vmem_limit_bytes=60 << 20
        ),
        name="fused",
    )(jnp.maximum(pick, 0), pos, back, bias, share, queries, output_grad, kv, ld)

    key_grad = jnp.transpose(kv_all[:, 0], (1, 0, 2))
    value_grad = jnp.transpose(kv_all[:, 1], (1, 0, 2))
    return query_grad, key_grad, value_grad


def solution(mesh):
    wide = P(("seq", "head"), None, None)
    return jax.shard_map(
        functools.partial(per_device, mesh.shape["seq"], mesh.shape["head"]),
        mesh=mesh,
        in_specs=(wide, wide, wide, wide, wide, P(("seq", "head"), None), P(), P()),
        out_specs=(wide, wide, wide),
        check_vma=False,
    )
```

profile of v0, /device:TPU:0, one launch (start us, length us, event | category | flops | bytes accessed | tf_op | source)
XLA Modules:
  0.0 158.6 jit_solution(6693717232584959541)
XLA Ops:
  0.7 0.8 copy.47
  1.4 0.1 reshape.78
  1.5 0.1 copy.48
  1.6 0.6 convert_reduce_fusion
  2.2 0.1 copy.49
  2.3 0.8 copy.50
  3.1 0.1 broadcast_in_dim_reshape.2
  3.2 0.1 select_reduce_fusion.1
  3.3 0.1 copy.51
  3.4 0.1 sub.13
  3.5 0.5 broadcast_maximum_fusion.pick
  4.0 0.6 fusion.2.share
  4.6 0.1 copy.61
  4.7 0.2 add_reduce_fusion
  4.9 0.0 copy-start.4
  4.9 0.6 select_reduce_fusion.back
  5.5 0.1 add.76
  5.6 0.1 fusion.3
  5.7 0.1 add_select_fusion
  5.8 0.6 select_n.25.bias
  6.4 0.0 copy-start.3
  6.4 0.0 copy-start.1
  6.4 0.0 copy-start.2
  6.4 3.7 %multiply_reduce_fusion = f32[288,32]{1,0:T(8,128)S(1)} fusion(bf16[288,32,128]{2,1,0:T(8,128)(2,1)} %param.11, bf16[288,32,128]{2,1,0:T(8,128)(2,1)} %g_in.1), kind=kLoop, calls=%fused_computation | loop fusion | flops 4709376 | bytes 4755456 | tf_op jit(solution)/shard_map/reduce_sum | solution.py:368
  10.1 0.0 copy-done.4
  10.1 0.1 copy.56
  10.2 0.0 copy-done.3
  10.3 0.0 copy-done.1
  10.3 0.0 copy-done.2
  10.3 0.1 copy_bitcast_fusion
  10.4 0.9 maximum_bitcast_fusion.kv_in
  11.2 0.4 copy.57
  11.6 1.2 reshape.80.ld_in
  12.8 141.3 %fused.1 = (bf16[288,32,128]{2,1,0:T(8,128)(2,1)}, bf16[4,2,288,128]{3,2,1,0:T(8,128)(2,1)}) custom-call(s32[32]{0:T(128)} %broadcast_maximum_fusion.pick, s32[27]{0:T(128)} %copy-done.4, s32[32]{0:T(128)} %select_reduce_fusion.back, f32[54]{0:T(128)} %select_n.25.bias, f32[9,32]{1,0:T(8,128)} %fusion.2.share, bf16[288,32,128]{2,1,0:T(8,128)(2,1)} %q_in.1, ...), custom_call_target="tpu_custom_call" | custom-call | tf_op jit(solution)/shard_map/fused/pallas_call | solution.py:415
  154.2 0.0 copy-start
  154.2 1.2 slice_bitcast_fusion
  155.4 0.9 copy.60
  156.3 0.9 copy.59
  157.2 0.0 copy-done
  157.2 1.4 copy.65
  (8 shorter events, 0.1 us)
Async XLA Ops:
  4.9 5.2 %copy-start.4 = (s32[27]{0:T(128)}, s32[27]{0:T(128)S(1)}, u32[]{:S(2)}) copy-start(s32[27]{0:T(128)S(1)} %get-tuple-element.23.pos) | copy-start | bytes 328
  6.4 3.9 %copy-start.3 = (f32[288,32]{0,1:T(8,128)S(1)}, f32[288,32]{0,1:T(8,128)}, u32[]{:S(2)}) copy-start(f32[288,32]{0,1:T(8,128)} %param.13) | copy-start | bytes 110596
  6.4 3.9 %copy-start.1 = (bf16[288,4,128]{2,1,0:T(4,128)(2,1)S(1)}, bf16[288,4,128]{2,1,0:T(4,128)(2,1)}, u32[]{:S(2)}) copy-start(bf16[288,4,128]{2,1,0:T(4,128)(2,1)} %param.10) | copy-start | bytes 884740
  6.4 3.9 %copy-start.2 = (bf16[288,4,128]{2,1,0:T(4,128)(2,1)S(1)}, bf16[288,4,128]{2,1,0:T(4,128)(2,1)}, u32[]{:S(2)}) copy-start(bf16[288,4,128]{2,1,0:T(4,128)(2,1)} %param.9) | copy-start | bytes 884740
  154.2 3.0 %copy-start = (bf16[288,32,128]{2,1,0:T(8,128)(2,1)S(1)}, bf16[288,32,128]{2,1,0:T(8,128)(2,1)}, u32[]{:S(2)}) copy-start(bf16[288,32,128]{2,1,0:T(8,128)(2,1)} %get-tuple-element.33) | copy-start | bytes 7077892
where the time goes:
time: 159 us
  Pallas kernels  141 us (89%)
  local copies, waits for them, and re-layouts  8.99 us (6%)
  other arithmetic  7.48 us (5%)
    pallas_call x1, Pallas kernels, per_device(): pl.pallas_call(functools.partial(fused, n_seq, n_head, most, blocks), out...  141 us
    unnamed x16, local copies, waits for them, and re-layouts  4.81 us
    reduce_sum x1, other arithmetic, per_device(): delta = jnp.sum(output_grad.astype(F32) * outputs.astype(F32), axis=-1)  3.73 us

commit v1 on v0

v1 whole, which is shorter than its diff:
```python
import functools
import math

import jax
import jax.numpy as jnp
from jax import lax
from jax.experimental import pallas as pl
from jax.experimental.pallas import tpu as pltpu
from jax.sharding import PartitionSpec as P

HD = 128
BLK = 128
G = 2
RND = 3
MESH = pl.DeviceIdType.MESH
F32 = jnp.float32
BF16 = jnp.bfloat16
LOG2E = math.log2(math.e)


def greet(n_seq, n_head, seq, head):
    barrier = pltpu.get_barrier_semaphore()

    def to_head(d, c):
        pl.semaphore_signal(
            barrier, inc=1, device_id={"head": lax.rem(head + d, n_head)}, device_id_type=MESH
        )
        return c

    def to_seq(d, c):
        pl.semaphore_signal(
            barrier, inc=1, device_id={"seq": lax.rem(seq + d, n_seq)}, device_id_type=MESH
        )
        return c

    lax.fori_loop(1, n_head, to_head, 0)
    lax.fori_loop(1, n_seq, to_seq, 0)
    pl.semaphore_wait(barrier, n_head + n_seq - 2)


def remote(src, dst, send, recv, **where):
    return pltpu.make_async_remote_copy(
        src_ref=src,
        dst_ref=dst,
        send_sem=send,
        recv_sem=recv,
        device_id=where,
        device_id_type=MESH,
    )


def loop(low, high, body):
    def run(i, c):
        body(i)
        return c

    lax.fori_loop(low, high, run, 0)


def dot(a, b, ca, cb):
    return lax.dot_general(a, b, (((ca,), (cb,)), ((), ())), preferred_element_type=F32)


def pair_grads(k, v, shifts, q, g, delta, scaling):
    scores = dot(k, q, 1, 1) * (scaling * LOG2E)
    weights = jnp.concatenate(
        [jnp.exp2(scores[i * BLK : (i + 1) * BLK] - shift) for i, shift in enumerate(shifts)],
        axis=0,
    )
    score_grad = (weights * (dot(v, g, 1, 1) - delta)).astype(BF16)
    dv = dot(weights.astype(BF16), g, 1, 0)
    dk = dot(score_grad, q, 1, 0) * scaling
    return dk, dv, dot(k, score_grad, 0, 0)


def arrival_order(n_head, toks, blocks, pieces):
    size = toks // pieces
    stages = []
    for b in range(blocks):
        stage = -1
        for part in range(b * BLK // size, (b * BLK + BLK - 1) // size + 1):
            if part // pieces >= n_head // 2:
                stage = max(stage, part % pieces)
        stages.append((stage, b))
    return sorted(stages)


def tables(n_seq, most, blocks, seq, owner, slot, pick, pos, back):
    entries = [(b, j) for b in range(blocks) for j in range(RND)]
    mine = [owner[seq * blocks + b, j] for b, j in entries]
    for e, own in enumerate(mine):
        rank = jnp.int32(0)
        for other in mine[:e]:
            rank = rank + jnp.where(other == own, 1, 0)
        pos[e] = own * most + rank

    def scan(names, values, wanted, table, at, empty):
        count = jnp.int32(0)
        found = [jnp.int32(empty)] * most
        for name, value in zip(names, values):
            hit = name == wanted
            for m in range(most):
                found[m] = jnp.where(jnp.logical_and(hit, count == m), value, found[m])
            count = count + jnp.where(hit, 1, 0)
        for m in range(most):
            table[at * most + m] = found[m]

    def asked(p):
        names = [owner[p * blocks + b, j] for b, j in entries]
        values = [slot[p * blocks + b, j] for b, j in entries]
        scan(names, values, seq, pick, p, -1)

    def answered(p):
        names = [owner[seq * blocks + b, j] for b, j in entries]
        scan(names, [jnp.int32(e) for e in range(len(entries))], p, back, p, 0)

    loop(0, n_seq, asked)
    loop(0, n_seq, answered)


def fused(
    n_seq, n_head, most, blocks, pieces,
    owner, slot, q_in, g_in, o_in, kv_in, lse_in,
    dq_out, kv_out,
    pick, pos, back,
    g_own, o_own, delta_own,
    q_all, g_all, lse_all, delta_all, kv_ext, glob, rand, picked, held, acc, gacc, dq_acc, dq_all,
    rpart, rback, halo_part, halo, gpart, gall, kv_sum,
    ls, os, ks, kr, ts, tr, qs, qr, ds, dr, es, er,
    ss, sr, ns, nr, hs, hr, gs, gr, ps, pr, rs, rr,
):
    seq, head = lax.axis_index("seq"), lax.axis_index("head")
    toks = kv_in.shape[2]
    group = q_in.shape[1] // n_head
    rows = toks * group
    span = n_head * toks
    lines = rows // 128
    step = BLK * group
    half = n_head // 2
    size = toks // pieces
    scaling = 1.0 / HD**0.5
    turn = head // half
    far_half = range(half, n_head)
    plan = arrival_order(n_head, toks, blocks, pieces)

    def partner(d):
        base = lax.rem(head + 2 * (d // 2), n_head)
        return base + (1 - 2 * lax.rem(base, 2)) if d % 2 else base

    sends = list(range(2, n_head)) + [1]
    here = pl.ds(pl.multiple_of(head * toks, toks), toks)
    kv_rows = pl.ds(pl.multiple_of(BLK + head * toks, 32), toks)
    line_rows = pl.ds(head * lines, lines)

    def heads_of(ref, peer):
        return ref.at[:, pl.ds(pl.multiple_of(peer * group, group), group), :]

    own = [
        pltpu.make_async_copy(kv_in.at[head, 0], kv_ext.at[0, kv_rows, :], ls.at[0]),
        pltpu.make_async_copy(kv_in.at[head, 1], kv_ext.at[1, kv_rows, :], ls.at[1]),
        pltpu.make_async_copy(lse_in.at[head], lse_all.at[line_rows], ls.at[2]),
        pltpu.make_async_copy(heads_of(q_in, head), q_all.at[here], ls.at[3]),
        pltpu.make_async_copy(heads_of(g_in, head), g_all.at[here], ls.at[4]),
    ]
    taken = [
        pltpu.make_async_copy(heads_of(src, p), dst.at[p], os.at[i, p])
        for p in range(n_head)
        for i, (src, dst) in enumerate(((g_in, g_own), (o_in, o_own)))
    ]
    for copy in taken + own:
        copy.start()

    greet(n_seq, n_head, seq, head)

    def kv_head(part, d):
        peer = partner(d)
        return remote(
            kv_in.at[peer, part], kv_ext.at[part, kv_rows, :], ks.at[part, d], kr.at[part, d], head=peer
        )

    def line_head(kind, d):
        peer = partner(d)
        src, dst = ((lse_in, lse_all), (delta_own, delta_all))[kind]
        return remote(src.at[peer], dst.at[line_rows], ts.at[kind, d], tr.at[kind, d], head=peer)

    def mirrored(side, i, n):
        return i + side * (n - 1 - 2 * i)

    def piece_send(kind, d, i):
        peer = partner(d)
        side = peer // half
        off = mirrored(side, i, pieces) * size
        src = (q_in, g_in)[kind].at[
            pl.ds(off, size), pl.ds(pl.multiple_of(peer * group, group), group), :
        ]
        dst = (q_all, g_all)[kind].at[pl.ds(head * toks + off, size)]
        return remote(
            src, dst, qs.at[kind, d, i], qr.at[kind, mirrored(side, head, n_head), i], head=peer
        )

    def piece_wait(kind, v, i):
        off = mirrored(turn, v, n_head) * toks + mirrored(turn, i, pieces) * size
        dst = (q_all, g_all)[kind].at[pl.ds(off, size)]
        remote(dst, dst, qs.at[kind, 0, i], qr.at[kind, v, i], head=partner(1)).wait_recv()

    for part in range(2):
        for d in sends:
            kv_head(part, d).start()
    for d in sends:
        line_head(0, d).start()
    for kind in range(2):
        for i in range(pieces):
            piece_send(kind, 1, i).start()

    for copy in taken:
        copy.wait()
    ones = jnp.ones((HD, 128), BF16)
    eye = (
        lax.broadcasted_iota(jnp.int32, (128, 128), 0)
        == lax.broadcasted_iota(jnp.int32, (128, 128), 1)
    ).astype(F32)
    cut = 32
    flat = cut * group
    for p in range(n_head):
        def row_delta(c):
            at = pl.ds(pl.multiple_of(c * cut, cut), cut)
            full = g_own[p, at].reshape(flat, HD).astype(F32) * o_own[p, at].reshape(flat, HD).astype(F32)
            high = full.astype(BF16)
            low = (full - high.astype(F32)).astype(BF16)
            sums = dot(high, ones, 1, 0) + dot(low, ones, 1, 0)
            for r in range(flat // 128):
                line = jnp.sum(sums[r * 128 : (r + 1) * 128] * eye, axis=0, keepdims=True)
                delta_own[p, c * (flat // 128) + r] = line

        loop(0, toks // cut, row_delta)
    delta_all[line_rows] = delta_own[head]
    for d in sends:
        line_head(1, d).start()
    for i in range(pieces):
        for kind in range(2):
            for d in range(2, n_head):
                piece_send(kind, d, i).start()
    tables(n_seq, most, blocks, seq, owner, slot, pick, pos, back)

    up, down = lax.rem(seq + 1, n_seq), lax.rem(seq + n_seq - 1, n_seq)

    def to_up(part):
        return remote(
            kv_ext.at[part, pl.ds(span, BLK), :], kv_ext.at[part, pl.ds(0, BLK), :],
            ns.at[part, 0], nr.at[part, 0], seq=up,
        )

    def to_down(part):
        return remote(
            kv_ext.at[part, pl.ds(BLK, BLK), :], kv_ext.at[part, pl.ds(BLK + span, BLK), :],
            ns.at[part, 1], nr.at[part, 1], seq=down,
        )

    def slots_of(peer):
        return pl.ds(peer * most, most)

    def rand_copy(part, d):
        peer = lax.rem(seq + d, n_seq)
        return remote(
            picked.at[part, slots_of(peer)], rand.at[part, slots_of(seq)],
            ss.at[part, d], sr.at[part, d], seq=peer,
        )

    def glob_copy(part, d):
        return remote(
            kv_ext.at[part, pl.ds(BLK, G * BLK), :], glob.at[part], gs.at[part, d], gr.at[part], seq=d
        )

    for part in range(2):
        own[part].wait()
        for d in range(1, n_head):
            kv_head(part, d).wait_recv()
        for block in range(blocks):
            held[part, block] = kv_ext[part, (block + 1) * BLK : (block + 2) * BLK, :]
        def fill(i):
            picked[part, i] = held[part, jnp.maximum(pick[i], 0)]

        loop(0, n_seq * most, fill)
        to_up(part).start()
        to_down(part).start()

        @pl.when(seq == 0)
        def _():
            loop(1, n_seq, lambda d: glob_copy(part, d).start())
            glob[part] = kv_ext[part, BLK : BLK + G * BLK, :]

        loop(1, n_seq, lambda d: rand_copy(part, d).start())
        rand[part, slots_of(seq)] = picked[part, slots_of(seq)]

    acc[...] = jnp.zeros_like(acc)
    gacc[...] = jnp.zeros_like(gacc)
    for part in range(2):
        to_up(part).wait()
        to_down(part).wait()

    @pl.when(seq > 0)
    def _():
        for part in range(2):
            glob_copy(part, 0).wait_recv()

    for copy in own[2:]:
        copy.wait()
    for kind in range(2):
        for d in range(1, n_head):
            line_head(kind, d).wait_recv()
        for k in range(1, half):
            v = lax.rem(mirrored(turn, head, n_head) + k, half)
            for i in range(pieces):
                piece_wait(kind, v, i)

    def landed(i):
        for kind in range(2):
            for v in far_half:
                piece_wait(kind, v, i)

    def block_at(i):
        b = jnp.int32(plan[0][1])
        for k in range(1, blocks):
            b = jnp.where(i == k, plan[k][1], b)
        return mirrored(turn, b, blocks)

    def operands(b):
        spot = pl.ds(pl.multiple_of(b * BLK, BLK), BLK)
        per = step // 128

        def lanes(ref):
            tile = ref[pl.ds(b * per, per)]
            return jnp.concatenate([tile[r] for r in range(per)], axis=1)

        flat = (step, HD)
        return q_all[spot].reshape(flat), g_all[spot].reshape(flat), lanes(lse_all) * LOG2E, lanes(delta_all)

    def hidden(okay):
        return jnp.where(okay, 0.0, 1e30).astype(F32)

    def near(i, fresh):
        b = block_at(i)
        q, g, lse, delta = operands(b)
        at = pl.multiple_of(b * BLK, BLK)
        win = pl.ds(at, 3 * BLK)
        dk, dv, dq = pair_grads(glob[0], glob[1], [lse] * G, q, g, delta, scaling)
        gacc[0] += dk
        gacc[1] += dv
        block = seq * blocks + b
        shifts = []
        for j in range(-1, 2):
            okay = jnp.logical_and(block + j >= G, block + j <= n_seq * blocks - 1)
            shifts.append(lse + hidden(okay))
        dk, dv, more = pair_grads(kv_ext[0, win, :], kv_ext[1, win, :], shifts, q, g, delta, scaling)
        acc[0, win, :] += dk
        acc[1, win, :] += dv
        if fresh:
            dq_acc[b] = dq + more
        else:
            total = dq_acc[b] + dq + more
            dq_all[pl.ds(at, BLK)] = (total.T * scaling).astype(BF16).reshape(BLK, group, HD)

    def far(i, fresh):
        b = block_at(i)
        q, g, lse, delta = operands(b)
        at = pl.multiple_of(b * BLK, BLK)
        block = seq * blocks + b
        k = jnp.concatenate([rand[0, pos[b * RND + j]] for j in range(RND)], axis=0)
        v = jnp.concatenate([rand[1, pos[b * RND + j]] for j in range(RND)], axis=0)
        shifts = []
        for j in range(RND):
            other = owner[block, j] * blocks + slot[block, j]
            okay = jnp.logical_and(other >= G, jnp.abs(other - block) >= 2)
            shifts.append(lse + hidden(okay))
        dk, dv, dq = pair_grads(k, v, shifts, q, g, delta, scaling)
        for j in range(RND):
            rpart[0, b * RND + j] = dk[j * BLK : (j + 1) * BLK].astype(BF16)
            rpart[1, b * RND + j] = dv[j * BLK : (j + 1) * BLK].astype(BF16)
        if fresh:
            dq_acc[b] = dq
        else:
            total = dq_acc[b] + dq
            dq_all[pl.ds(at, BLK)] = (total.T * scaling).astype(BF16).reshape(BLK, group, HD)

    last = pieces - 1
    early = sum(stage < last for stage, _ in plan)
    firsts = {}
    for i, (stage, _) in enumerate(plan):
        for s in range(stage + 1):
            firsts.setdefault(s, i)

    def near_early(i):
        for s in range(last):
            if s in firsts and firsts[s] < early:
                @pl.when(i == firsts[s])
                def _():
                    landed(s)

        near(i, True)

    loop(0, early, near_early)
    for s in range(last):
        if s not in firsts or firsts[s] >= early:
            landed(s)
    for part in range(2):
        loop(1, n_seq, lambda d: rand_copy(part, d).wait())
    loop(0, early, lambda i: far(i, False))
    landed(last)
    loop(early, blocks, lambda i: far(i, True))

    def back_copy(part, d):
        peer = lax.rem(seq + d, n_seq)
        return remote(
            picked.at[part, slots_of(peer)], rback.at[part, slots_of(seq)],
            rs.at[part, d], rr.at[part, d], seq=peer,
        )

    def gather(part):
        def move(i):
            picked[part, i] = rpart[part, back[i]]

        loop(0, n_seq * most, move)

    gather(1)
    loop(1, n_seq, lambda d: back_copy(1, d).start())
    loop(early, blocks, lambda i: near(i, False))

    halo_part[0] = acc[:, 0:BLK, :].astype(BF16)
    halo_part[1] = acc[:, BLK + span :, :].astype(BF16)
    gpart[...] = gacc[...].astype(BF16)

    def dq_copy(d):
        peer = partner(d)
        src = dq_all.at[pl.ds(pl.multiple_of(peer * toks, toks), toks)]
        return remote(src, heads_of(dq_out, head), ds.at[d], dr.at[d], head=peer)

    def kv_copy(part, d):
        peer = partner(d)
        src = kv_sum.at[part, pl.ds(pl.multiple_of(peer * toks, 32), toks), :]
        return remote(src, kv_out.at[head, part], es.at[part, d], er.at[part, d], head=peer)

    def part_copy():
        return remote(gpart, gall.at[seq], ps.at[0], pr.at[seq], seq=0)

    down_grad = remote(halo_part.at[0], halo.at[0], hs.at[0], hr.at[0], seq=down)
    up_grad = remote(halo_part.at[1], halo.at[1], hs.at[1], hr.at[1], seq=up)
    down_grad.start()
    up_grad.start()

    @pl.when(seq > 0)
    def _():
        part_copy().start()

    gather(0)
    loop(1, n_seq, lambda d: back_copy(0, d).start())
    own_dq = pltpu.make_async_copy(dq_all.at[here], heads_of(dq_out, head), ls.at[5])
    for d in sends:
        dq_copy(d).start()
    own_dq.start()
    for part in range(2):
        rback[part, slots_of(seq)] = picked[part, slots_of(seq)]

    for d in range(1, n_head):
        for kind in range(2):
            kv_head(kind, d).wait_send()
            line_head(kind, d).wait_send()
            for i in range(pieces):
                piece_send(kind, d, i).wait_send()

    def absorb(part, d):
        base = lax.rem(seq + n_seq - d, n_seq) * most

        def block_sum(block):
            over = pl.ds(pl.multiple_of(block * BLK + BLK, BLK), BLK)
            value = acc[part, over, :]
            for m in range(most):
                share = jnp.where(pick[base + m] == block, 1.0, 0.0).astype(F32)
                value = value + share * rback[part, base + m].astype(F32)
            acc[part, over, :] = value

        loop(0, blocks, block_sum)

    absorb(1, 0)
    absorb(0, 0)

    @pl.when(seq == 0)
    def _():
        for part in range(2):
            loop(1, n_seq, lambda d: glob_copy(part, d).wait_send())
        gall[0] = gpart[...]

    for part in (1, 0):
        def take(d):
            back_copy(part, d).wait()
            absorb(part, d)

        loop(1, n_seq, take)
        if part:
            @pl.when(seq == 0)
            def _():
                def arrive(d):
                    remote(gpart, gall.at[d], ps.at[0], pr.at[d], seq=0).wait_recv()

                loop(1, n_seq, arrive)

                def add(d):
                    gacc[...] += gall[d].astype(F32)

                loop(1, n_seq, add)
                acc[:, BLK : BLK + G * BLK, :] += gacc[...]

            @pl.when(seq > 0)
            def _():
                part_copy().wait_send()

            down_grad.wait()
            up_grad.wait()
            acc[:, BLK : 2 * BLK, :] += halo[1].astype(F32)
            acc[:, span : span + BLK, :] += halo[0].astype(F32)
        kv_sum[part] = acc[part, BLK : BLK + span, :].astype(BF16)
        for d in sends:
            kv_copy(part, d).start()
        kv_out[head, part] = kv_sum[part, pl.ds(pl.multiple_of(head * toks, 32), toks), :]
    own_dq.wait()
    for d in range(1, n_head):
        dq_copy(d).wait()
    for part in range(2):
        for d in range(1, n_head):
            kv_copy(part, d).wait()


def per_device(
    n_seq, n_head,
    queries, key_states, value_states, outputs, output_grad, logsumexp, random_owner, random_slot,
):
    toks, heads, _ = queries.shape
    group = heads // n_head
    rows = toks * group
    span = toks * n_head
    blocks = span // BLK
    per_row = blocks * RND
    most = max(1, (per_row + n_seq - 1) // n_seq)
    pieces = 3 if toks % 3 == 0 else 1
    vmem = pl.BlockSpec(memory_space=pltpu.VMEM)
    smem = pl.BlockSpec(memory_space=pltpu.SMEM)
    hbm = pl.BlockSpec(memory_space=pl.ANY)
    dma = pltpu.SemaphoreType.DMA

    lse = jnp.transpose(logsumexp.reshape(toks, n_head, group), (1, 0, 2))
    lse = lse.reshape(n_head, rows // 128, 1, 128)
    kv = jnp.transpose(jnp.stack([key_states, value_states]), (2, 0, 1, 3))

    slots = n_seq * most
    step = BLK * group
    query_grad, kv_all = pl.pallas_call(
        functools.partial(fused, n_seq, n_head, most, blocks, pieces),
        out_shape=[
            jax.ShapeDtypeStruct((toks, heads, HD), BF16),
            jax.ShapeDtypeStruct((n_head, 2, toks, HD), BF16),
        ],
        in_specs=[smem, smem, hbm, hbm, hbm, vmem, vmem],
        out_specs=[hbm, vmem],
        scratch_shapes=[
            pltpu.SMEM((slots,), jnp.int32),
            pltpu.SMEM((per_row,), jnp.int32),
            pltpu.SMEM((slots,), jnp.int32),
            pltpu.VMEM((n_head, toks, group, HD), BF16),
            pltpu.VMEM((n_head, toks, group, HD), BF16),
            pltpu.VMEM((n_head, rows // 128, 1, 128), F32),
            pltpu.VMEM((span, group, HD), BF16),
            pltpu.VMEM((span, group, HD), BF16),
            pltpu.VMEM((n_head * rows // 128, 1, 128), F32),
            pltpu.VMEM((n_head * rows // 128, 1, 128), F32),
            pltpu.VMEM((2, span + 2 * BLK, HD), BF16),
            pltpu.VMEM((2, G * BLK, HD), BF16),
            pltpu.VMEM((2, slots, BLK, HD), BF16),
            pltpu.VMEM((2, slots, BLK, HD), BF16),
            pltpu.VMEM((2, blocks, BLK, HD), BF16),
            pltpu.VMEM((2, span + 2 * BLK, HD), F32),
            pltpu.VMEM((2, G * BLK, HD), F32),
            pltpu.VMEM((blocks, HD, step), F32),
            pltpu.VMEM((span, group, HD), BF16),
            pltpu.VMEM((2, per_row, BLK, HD), BF16),
            pltpu.VMEM((2, slots, BLK, HD), BF16),
            pltpu.VMEM((2, 2, BLK, HD), BF16),
            pltpu.VMEM((2, 2, BLK, HD), BF16),
            pltpu.VMEM((2, G * BLK, HD), BF16),
            pltpu.VMEM((n_seq, 2, G * BLK, HD), BF16),
            pltpu.VMEM((2, span, HD), BF16),
            dma((6,)), dma((2, n_head)), dma((2, n_head)), dma((2, n_head)),
            dma((2, n_head)), dma((2, n_head)),
            dma((2, n_head, pieces)), dma((2, n_head, pieces)),
            dma((n_head,)), dma((n_head,)), dma((2, n_head)), dma((2, n_head)),
            dma((2, n_seq)), dma((2, n_seq)), dma((2, 2)), dma((2, 2)), dma((2,)), dma((2,)),
            dma((2, n_seq)), dma((2,)), dma((1,)), dma((n_seq,)),
            dma((2, n_seq)), dma((2, n_seq)),
        ],
        compiler_params=pltpu.CompilerParams(
            collective_id=0, has_side_effects=True, vmem_limit_bytes=60 << 20
        ),
        name="fused",
    )(random_owner, random_slot, queries, output_grad, outputs, kv, lse)

    key_grad = jnp.transpose(kv_all[:, 0], (1, 0, 2))
    value_grad = jnp.transpose(kv_all[:, 1], (1, 0, 2))
    return query_grad, key_grad, value_grad


def solution(mesh):
    wide = P(("seq", "head"), None, None)
    return jax.shard_map(
        functools.partial(per_device, mesh.shape["seq"], mesh.shape["head"]),
        mesh=mesh,
        in_specs=(wide, wide, wide, wide, wide, P(("seq", "head"), None), P(), P()),
        out_specs=(wide, wide, wide),
        check_vma=False,
    )
```

time: 159 us -> 152 us (0.956)
  the two profiles are of different devices: /device:TPU:0 before, /device:TPU:27 now
where the time goes in v1:
time: 152 us; the launch traced here: 151 us
  Pallas kernels  139 us (91%)
  local copies, waits for them, and re-layouts  10.2 us (7%)
    pallas_call x1, Pallas kernels, per_device(): pl.pallas_call(functools.partial(fused, n_seq, n_head, most, blocks, piec...  139 us
    unnamed x7, local copies, waits for them, and re-layouts  5.92 us

profile of v1, /device:TPU:27, one launch (start us, length us, event | category | flops | bytes accessed | tf_op | source)
XLA Modules:
  0.0 151.2 jit_solution(15371375860167746587)
XLA Ops:
  0.6 1.4 copy.21.owner
  2.0 1.4 copy.22.slot
  3.4 1.0 copy.20
  4.4 0.9 reshape.14.lse_in
  5.4 1.1 copy_bitcast_fusion
  6.5 0.9 maximum_bitcast_fusion.kv_in
  7.4 139.5 %fused.1 = (bf16[288,32,128]{2,1,0:T(8,128)(2,1)}, bf16[4,2,288,128]{3,2,1,0:T(8,128)(2,1)}) custom-call(s32[72,3]{1,0:T(8,128)} %copy.21.owner, s32[72,3]{1,0:T(8,128)} %copy.22.slot, bf16[288,32,128]{2,1,0:T(8,128)(2,1)} %q_in.1, bf16[288,32,128]{2,1,0:T(8,128)(2,1)} %g_in.1, bf16[288,32,128]{2,1,0:T(8,128)(2,1)} %o_in.1, ...), custom_call_target="tpu_custom_call" | custom-call | tf_op jit(solution)/shard_map/fused/pallas_call | solution.py:555
  146.8 0.0 copy-start
  146.8 1.2 slice_bitcast_fusion
  148.1 0.9 copy.25
  148.9 0.9 copy.24
  149.8 0.0 copy-done
  149.8 1.4 copy.29
Async XLA Ops:
  146.8 3.0 %copy-start = (bf16[288,32,128]{2,1,0:T(8,128)(2,1)S(1)}, bf16[288,32,128]{2,1,0:T(8,128)(2,1)}, u32[]{:S(2)}) copy-start(bf16[288,32,128]{2,1,0:T(8,128)(2,1)} %get-tuple-element.20) | copy-start | bytes 7077892

commit v2 on v1

--- a/solution.py
+++ b/solution.py
@@ -87,7 +87,7 @@
 
 def tables(n_seq, most, blocks, seq, owner, slot, pick, pos, back):
     entries = [(b, j) for b in range(blocks) for j in range(RND)]
-    mine = [owner[seq * blocks + b, j] for b, j in entries]
+    mine = [owner[j, seq * blocks + b] for b, j in entries]
     for e, own in enumerate(mine):
         rank = jnp.int32(0)
         for other in mine[:e]:
@@ -106,12 +106,12 @@
             table[at * most + m] = found[m]
 
     def asked(p):
-        names = [owner[p * blocks + b, j] for b, j in entries]
-        values = [slot[p * blocks + b, j] for b, j in entries]
+        names = [owner[j, p * blocks + b] for b, j in entries]
+        values = [slot[j, p * blocks + b] for b, j in entries]
         scan(names, values, seq, pick, p, -1)
 
     def answered(p):
-        names = [owner[seq * blocks + b, j] for b, j in entries]
+        names = [owner[j, seq * blocks + b] for b, j in entries]
         scan(names, [jnp.int32(e) for e in range(len(entries))], p, back, p, 0)
 
     loop(0, n_seq, asked)
@@ -123,8 +123,8 @@
     owner, slot, q_in, g_in, o_in, kv_in, lse_in,
     dq_out, kv_out,
     pick, pos, back,
-    g_own, o_own, delta_own,
-    q_all, g_all, lse_all, delta_all, kv_ext, glob, rand, picked, held, acc, gacc, dq_acc, dq_all,
+    far_weights, g_own, o_own, delta_own,
+    q_all, g_all, lse_all, delta_all, kv_ext, glob, rand_k, rand_v, picked, held, acc, gacc, dq_acc, dq_all,
     rpart, rback, halo_part, halo, gpart, gall, kv_sum,
     ls, os, ks, kr, ts, tr, qs, qr, ds, dr, es, er,
     ss, sr, ns, nr, hs, hr, gs, gr, ps, pr, rs, rr,
@@ -141,6 +141,7 @@
     scaling = 1.0 / HD**0.5
     turn = head // half
     far_half = range(half, n_head)
+    rand = (rand_k, rand_v)
     plan = arrival_order(n_head, toks, blocks, pieces)
 
     def partner(d):
@@ -211,6 +212,61 @@
     for kind in range(2):
         for i in range(pieces):
             piece_send(kind, 1, i).start()
+    for kind in range(2):
+        for d in range(2, n_head):
+            piece_send(kind, d, 0).start()
+
+    tables(n_seq, most, blocks, seq, owner, slot, pick, pos, back)
+
+    up, down = lax.rem(seq + 1, n_seq), lax.rem(seq + n_seq - 1, n_seq)
+
+    def to_up(part):
+        return remote(
+            kv_ext.at[part, pl.ds(span, BLK), :], kv_ext.at[part, pl.ds(0, BLK), :],
+            ns.at[part, 0], nr.at[part, 0], seq=up,
+        )
+
+    def to_down(part):
+        return remote(
+            kv_ext.at[part, pl.ds(BLK, BLK), :], kv_ext.at[part, pl.ds(BLK + span, BLK), :],
+            ns.at[part, 1], nr.at[part, 1], seq=down,
+        )
+
+    def slots_of(peer):
+        return pl.ds(peer * most, most)
+
+    def rand_copy(part, d):
+        peer = lax.rem(seq + d, n_seq)
+        return remote(
+            picked.at[part, slots_of(peer)], rand[part].at[slots_of(seq)],
+            ss.at[part, d], sr.at[part, d], seq=peer,
+        )
+
+    def glob_copy(part, d):
+        return remote(
+            kv_ext.at[part, pl.ds(BLK, G * BLK), :], glob.at[part], gs.at[part, d], gr.at[part], seq=d
+        )
+
+    for part in range(2):
+        own[part].wait()
+        for d in range(1, n_head):
+            kv_head(part, d).wait_recv()
+        for block in range(blocks):
+            held[part, block] = kv_ext[part, (block + 1) * BLK : (block + 2) * BLK, :]
+        def fill(i):
+            picked[part, i] = held[part, jnp.maximum(pick[i], 0)]
+
+        loop(0, n_seq * most, fill)
+        to_up(part).start()
+        to_down(part).start()
+
+        @pl.when(seq == 0)
+        def _():
+            loop(1, n_seq, lambda d: glob_copy(part, d).start())
+            glob[part] = kv_ext[part, BLK : BLK + G * BLK, :]
+
+        loop(1, n_seq, lambda d: rand_copy(part, d).start())
+        rand[part][slots_of(seq)] = picked[part, slots_of(seq)]
 
     for copy in taken:
         copy.wait()
@@ -236,61 +292,10 @@
     delta_all[line_rows] = delta_own[head]
     for d in sends:
         line_head(1, d).start()
-    for i in range(pieces):
+    for i in range(1, pieces):
         for kind in range(2):
             for d in range(2, n_head):
                 piece_send(kind, d, i).start()
-    tables(n_seq, most, blocks, seq, owner, slot, pick, pos, back)
-
-    up, down = lax.rem(seq + 1, n_seq), lax.rem(seq + n_seq - 1, n_seq)
-
-    def to_up(part):
-        return remote(
-            kv_ext.at[part, pl.ds(span, BLK), :], kv_ext.at[part, pl.ds(0, BLK), :],
-            ns.at[part, 0], nr.at[part, 0], seq=up,
-        )
-
-    def to_down(part):
-        return remote(
-            kv_ext.at[part, pl.ds(BLK, BLK), :], kv_ext.at[part, pl.ds(BLK + span, BLK), :],
-            ns.at[part, 1], nr.at[part, 1], seq=down,
-        )
-
-    def slots_of(peer):
-        return pl.ds(peer * most, most)
-
-    def rand_copy(part, d):
-        peer = lax.rem(seq + d, n_seq)
-        return remote(
-            picked.at[part, slots_of(peer)], rand.at[part, slots_of(seq)],
-            ss.at[part, d], sr.at[part, d], seq=peer,
-        )
-
-    def glob_copy(part, d):
-        return remote(
-            kv_ext.at[part, pl.ds(BLK, G * BLK), :], glob.at[part], gs.at[part, d], gr.at[part], seq=d
-        )
-
-    for part in range(2):
-        own[part].wait()
-        for d in range(1, n_head):
-            kv_head(part, d).wait_recv()
-        for block in range(blocks):
-            held[part, block] = kv_ext[part, (block + 1) * BLK : (block + 2) * BLK, :]
-        def fill(i):
-            picked[part, i] = held[part, jnp.maximum(pick[i], 0)]
-
-        loop(0, n_seq * most, fill)
-        to_up(part).start()
-        to_down(part).start()
-
-        @pl.when(seq == 0)
-        def _():
-            loop(1, n_seq, lambda d: glob_copy(part, d).start())
-            glob[part] = kv_ext[part, BLK : BLK + G * BLK, :]
-
-        loop(1, n_seq, lambda d: rand_copy(part, d).start())
-        rand[part, slots_of(seq)] = picked[part, slots_of(seq)]
 
     acc[...] = jnp.zeros_like(acc)
     gacc[...] = jnp.zeros_like(gacc)
@@ -305,15 +310,22 @@
 
     for copy in own[2:]:
         copy.wait()
+    soon = [1] if half == 2 else list(range(1, n_head))
+    for d in range(1, n_head):
+        line_head(0, d).wait_recv()
+    for d in soon:
+        line_head(1, d).wait_recv()
     for kind in range(2):
-        for d in range(1, n_head):
-            line_head(kind, d).wait_recv()
         for k in range(1, half):
             v = lax.rem(mirrored(turn, head, n_head) + k, half)
             for i in range(pieces):
                 piece_wait(kind, v, i)
 
     def landed(i):
+        if i == 0:
+            for d in range(1, n_head):
+                if d not in soon:
+                    line_head(1, d).wait_recv()
         for kind in range(2):
             for v in far_half:
                 piece_wait(kind, v, i)
@@ -338,7 +350,7 @@
     def hidden(okay):
         return jnp.where(okay, 0.0, 1e30).astype(F32)
 
-    def near(i, fresh):
+    def near(i):
         b = block_at(i)
         q, g, lse, delta = operands(b)
         at = pl.multiple_of(b * BLK, BLK)
@@ -354,33 +366,39 @@
         dk, dv, more = pair_grads(kv_ext[0, win, :], kv_ext[1, win, :], shifts, q, g, delta, scaling)
         acc[0, win, :] += dk
         acc[1, win, :] += dv
-        if fresh:
-            dq_acc[b] = dq + more
-        else:
-            total = dq_acc[b] + dq + more
-            dq_all[pl.ds(at, BLK)] = (total.T * scaling).astype(BF16).reshape(BLK, group, HD)
-
-    def far(i, fresh):
+        dq_acc[b] = dq + more
+
+    def found(part, b):
+        return jnp.concatenate([rand[part][pos[b * RND + j]] for j in range(RND)], axis=0)
+
+    def far_values(i):
         b = block_at(i)
-        q, g, lse, delta = operands(b)
+        q, g, lse, _ = operands(b)
+        block = seq * blocks + b
+        scores = dot(found(0, b), q, 1, 1) * (scaling * LOG2E)
+        parts = []
+        for j in range(RND):
+            other = owner[j, block] * blocks + slot[j, block]
+            okay = jnp.logical_and(other >= G, jnp.abs(other - block) >= 2)
+            shift = lse + hidden(okay)
+            parts.append(jnp.exp2(scores[j * BLK : (j + 1) * BLK] - shift).astype(BF16))
+        weights = jnp.concatenate(parts, axis=0)
+        far_weights[b] = weights
+        dv = dot(weights, g, 1, 0)
+        for j in range(RND):
+            rpart[1, b * RND + j] = dv[j * BLK : (j + 1) * BLK].astype(BF16)
+
+    def far_keys(i):
+        b = block_at(i)
+        q, g, _, delta = operands(b)
         at = pl.multiple_of(b * BLK, BLK)
-        block = seq * blocks + b
-        k = jnp.concatenate([rand[0, pos[b * RND + j]] for j in range(RND)], axis=0)
-        v = jnp.concatenate([rand[1, pos[b * RND + j]] for j in range(RND)], axis=0)
-        shifts = []
-        for j in range(RND):
-            other = owner[block, j] * blocks + slot[block, j]
-            okay = jnp.logical_and(other >= G, jnp.abs(other - block) >= 2)
-            shifts.append(lse + hidden(okay))
-        dk, dv, dq = pair_grads(k, v, shifts, q, g, delta, scaling)
+        rise = dot(found(1, b), g, 1, 1) - delta
+        score_grad = (far_weights[b].astype(F32) * rise).astype(BF16)
+        dk = dot(score_grad, q, 1, 0) * scaling
         for j in range(RND):
             rpart[0, b * RND + j] = dk[j * BLK : (j + 1) * BLK].astype(BF16)
-            rpart[1, b * RND + j] = dv[j * BLK : (j + 1) * BLK].astype(BF16)
-        if fresh:
-            dq_acc[b] = dq
-        else:
-            total = dq_acc[b] + dq
-            dq_all[pl.ds(at, BLK)] = (total.T * scaling).astype(BF16).reshape(BLK, group, HD)
+        total = dq_acc[b] + dot(found(0, b), score_grad, 0, 0)
+        dq_all[pl.ds(at, BLK)] = (total.T * scaling).astype(BF16).reshape(BLK, group, HD)
 
     last = pieces - 1
     early = sum(stage < last for stage, _ in plan)
@@ -396,17 +414,17 @@
                 def _():
                     landed(s)
 
-        near(i, True)
+        near(i)
 
     loop(0, early, near_early)
     for s in range(last):
         if s not in firsts or firsts[s] >= early:
             landed(s)
-    for part in range(2):
-        loop(1, n_seq, lambda d: rand_copy(part, d).wait())
-    loop(0, early, lambda i: far(i, False))
+    loop(1, n_seq, lambda d: rand_copy(0, d).wait())
+    loop(0, early, far_values)
     landed(last)
-    loop(early, blocks, lambda i: far(i, True))
+    loop(early, blocks, far_values)
+    loop(1, n_seq, lambda d: rand_copy(1, d).wait_send())
 
     def back_copy(part, d):
         peer = lax.rem(seq + d, n_seq)
@@ -423,7 +441,7 @@
 
     gather(1)
     loop(1, n_seq, lambda d: back_copy(1, d).start())
-    loop(early, blocks, lambda i: near(i, False))
+    loop(early, blocks, near)
 
     halo_part[0] = acc[:, 0:BLK, :].astype(BF16)
     halo_part[1] = acc[:, BLK + span :, :].astype(BF16)
@@ -451,6 +469,8 @@
     def _():
         part_copy().start()
 
+    loop(1, n_seq, lambda d: rand_copy(1, d).wait_recv())
+    loop(0, blocks, far_keys)
     gather(0)
     loop(1, n_seq, lambda d: back_copy(0, d).start())
     own_dq = pltpu.make_async_copy(dq_all.at[here], heads_of(dq_out, head), ls.at[5])
@@ -564,6 +584,7 @@
             pltpu.SMEM((slots,), jnp.int32),
             pltpu.SMEM((per_row,), jnp.int32),
             pltpu.SMEM((slots,), jnp.int32),
+            pltpu.VMEM((blocks, RND * BLK, step), BF16),
             pltpu.VMEM((n_head, toks, group, HD), BF16),
             pltpu.VMEM((n_head, toks, group, HD), BF16),
             pltpu.VMEM((n_head, rows // 128, 1, 128), F32),
@@ -573,7 +594,8 @@
             pltpu.VMEM((n_head * rows // 128, 1, 128), F32),
             pltpu.VMEM((2, span + 2 * BLK, HD), BF16),
             pltpu.VMEM((2, G * BLK, HD), BF16),
-            pltpu.VMEM((2, slots, BLK, HD), BF16),
+            pltpu.VMEM((slots, BLK, HD), BF16),
+            pltpu.VMEM((slots, BLK, HD), BF16),
             pltpu.VMEM((2, slots, BLK, HD), BF16),
             pltpu.VMEM((2, blocks, BLK, HD), BF16),
             pltpu.VMEM((2, span + 2 * BLK, HD), F32),
@@ -599,7 +621,7 @@
             collective_id=0, has_side_effects=True, vmem_limit_bytes=60 << 20
         ),
         name="fused",
-    )(random_owner, random_slot, queries, output_grad, outputs, kv, lse)
+    )(random_owner.T, random_slot.T, queries, output_grad, outputs, kv, lse)
 
     key_grad = jnp.transpose(kv_all[:, 0], (1, 0, 2))
     value_grad = jnp.transpose(kv_all[:, 1], (1, 0, 2))

time: 152 us -> 136 us (0.89)
  the two profiles are of different devices: /device:TPU:27 before, /device:TPU:11 now
where the time goes in v2:
time: 136 us
  Pallas kernels  127 us (93%)
  local copies, waits for them, and re-layouts  7.47 us (5%)
    pallas_call x1, Pallas kernels, per_device(): pl.pallas_call(functools.partial(fused, n_seq, n_head, most, blocks, piec...  127 us
    unnamed x5, local copies, waits for them, and re-layouts  3.14 us

profile of v2, /device:TPU:11, one launch (start us, length us, event | category | flops | bytes accessed | tf_op | source)
XLA Modules:
  0.0 135.9 jit_solution(1946195796043375626)
XLA Ops:
  0.6 1.0 copy.18
  1.6 0.9 reshape.14.lse_in
  2.6 1.1 copy_bitcast_fusion
  3.7 0.9 maximum_bitcast_fusion.kv_in
  4.6 126.9 %fused.1 = (bf16[288,32,128]{2,1,0:T(8,128)(2,1)}, bf16[4,2,288,128]{3,2,1,0:T(8,128)(2,1)}) custom-call(s32[3,72]{1,0:T(4,128)} %bitcast.20, s32[3,72]{1,0:T(4,128)} %bitcast.21, bf16[288,32,128]{2,1,0:T(8,128)(2,1)} %q_in.1, bf16[288,32,128]{2,1,0:T(8,128)(2,1)} %g_in.1, bf16[288,32,128]{2,1,0:T(8,128)(2,1)} %o_in.1, ...), custom_call_target="tpu_custom_call" | custom-call | tf_op jit(solution)/shard_map/fused/pallas_call | solution.py:575
  131.5 0.0 copy-start
  131.5 1.2 slice_bitcast_fusion
  132.7 0.9 copy.21
  133.6 0.9 copy.20
  134.4 0.0 copy-done
  134.4 1.4 %copy.25 = bf16[288,32,128]{2,1,0:T(8,128)(2,1)} copy(bf16[288,32,128]{2,1,0:T(8,128)(2,1)S(1)} %copy-done) | data formatting | bytes 4718592
Async XLA Ops:
  131.5 3.0 %copy-start = (bf16[288,32,128]{2,1,0:T(8,128)(2,1)S(1)}, bf16[288,32,128]{2,1,0:T(8,128)(2,1)}, u32[]{:S(2)}) copy-start(bf16[288,32,128]{2,1,0:T(8,128)(2,1)} %get-tuple-element.20) | copy-start | bytes 7077892

commit v3 on v2

--- a/solution.py
+++ b/solution.py
@@ -120,9 +120,9 @@
 
 def fused(
     n_seq, n_head, most, blocks, pieces,
-    owner, slot, q_in, g_in, o_in, kv_in, lse_in,
-    dq_out, kv_out,
-    pick, pos, back,
+    owner, slot, q_in, g_in, o_in, k_raw, v_raw, lse_in,
+    dq_out, dk_out, dv_out,
+    kv_in, kv_out, lse_own, pick, pos, back,
     far_weights, g_own, o_own, delta_own,
     q_all, g_all, lse_all, delta_all, kv_ext, glob, rand_k, rand_v, picked, held, acc, gacc, dq_acc, dq_all,
     rpart, rback, halo_part, halo, gpart, gall, kv_sum,
@@ -159,7 +159,7 @@
     own = [
         pltpu.make_async_copy(kv_in.at[head, 0], kv_ext.at[0, kv_rows, :], ls.at[0]),
         pltpu.make_async_copy(kv_in.at[head, 1], kv_ext.at[1, kv_rows, :], ls.at[1]),
-        pltpu.make_async_copy(lse_in.at[head], lse_all.at[line_rows], ls.at[2]),
+        None,
         pltpu.make_async_copy(heads_of(q_in, head), q_all.at[here], ls.at[3]),
         pltpu.make_async_copy(heads_of(g_in, head), g_all.at[here], ls.at[4]),
     ]
@@ -168,9 +168,18 @@
         for p in range(n_head)
         for i, (src, dst) in enumerate(((g_in, g_own), (o_in, o_own)))
     ]
-    for copy in taken + own:
+    for copy in taken + own[3:]:
         copy.start()
 
+    def spread(part):
+        whole = (k_raw, v_raw)[part][...].astype(F32).reshape(toks, n_head * HD).astype(BF16)
+        for p in range(n_head):
+            kv_in[p, part] = whole[:, p * HD : (p + 1) * HD]
+
+    spread(0)
+    spread(1)
+    for copy in own[:2]:
+        copy.start()
     greet(n_seq, n_head, seq, head)
 
     def kv_head(part, d):
@@ -181,7 +190,7 @@
 
     def line_head(kind, d):
         peer = partner(d)
-        src, dst = ((lse_in, lse_all), (delta_own, delta_all))[kind]
+        src, dst = ((lse_own, lse_all), (delta_own, delta_all))[kind]
         return remote(src.at[peer], dst.at[line_rows], ts.at[kind, d], tr.at[kind, d], head=peer)
 
     def mirrored(side, i, n):
@@ -207,8 +216,6 @@
     for part in range(2):
         for d in sends:
             kv_head(part, d).start()
-    for d in sends:
-        line_head(0, d).start()
     for kind in range(2):
         for i in range(pieces):
             piece_send(kind, 1, i).start()
@@ -289,9 +296,27 @@
                 delta_own[p, c * (flat // 128) + r] = line
 
         loop(0, toks // cut, row_delta)
+    per_line = 128 // group
+    lane = lax.broadcasted_iota(jnp.int32, (per_line, 128), 1)
+    term = (lane // group == lax.broadcasted_iota(jnp.int32, (per_line, 128), 0)).astype(BF16)
+    terms = jnp.concatenate([term] * 3, axis=0)
+    wide = lax.broadcasted_iota(jnp.int32, (n_head * group, 128), 0)
+    keep = wide % group == lax.broadcasted_iota(jnp.int32, (n_head * group, 128), 1) % group
+    for r in range(toks // per_line):
+        full = lse_in[:, r * per_line : (r + 1) * per_line]
+        high = full.astype(BF16)
+        rest = full - high.astype(F32)
+        middle = rest.astype(BF16)
+        low = (rest - middle.astype(F32)).astype(BF16)
+        sums = dot(jnp.concatenate([high, middle, low], axis=1), terms, 1, 0)
+        sums = jnp.where(keep, sums, 0.0)
+        for p in range(n_head):
+            lse_own[p, r] = jnp.sum(sums[p * group : (p + 1) * group], axis=0, keepdims=True)
+    lse_all[line_rows] = lse_own[head]
     delta_all[line_rows] = delta_own[head]
     for d in sends:
-        line_head(1, d).start()
+        for kind in range(2):
+            line_head(kind, d).start()
     for i in range(1, pieces):
         for kind in range(2):
             for d in range(2, n_head):
@@ -308,13 +333,12 @@
         for part in range(2):
             glob_copy(part, 0).wait_recv()
 
-    for copy in own[2:]:
+    for copy in own[3:]:
         copy.wait()
     soon = [1] if half == 2 else list(range(1, n_head))
-    for d in range(1, n_head):
-        line_head(0, d).wait_recv()
     for d in soon:
-        line_head(1, d).wait_recv()
+        for kind in range(2):
+            line_head(kind, d).wait_recv()
     for kind in range(2):
         for k in range(1, half):
             v = lax.rem(mirrored(turn, head, n_head) + k, half)
@@ -325,6 +349,7 @@
         if i == 0:
             for d in range(1, n_head):
                 if d not in soon:
+                    line_head(0, d).wait_recv()
                     line_head(1, d).wait_recv()
         for kind in range(2):
             for v in far_half:
@@ -509,6 +534,12 @@
             loop(1, n_seq, lambda d: glob_copy(part, d).wait_send())
         gall[0] = gpart[...]
 
+    def finish(part):
+        for d in range(1, n_head):
+            kv_copy(part, d).wait()
+        whole = jnp.concatenate([kv_out[p, part] for p in range(n_head)], axis=1).astype(F32)
+        (dk_out, dv_out)[part][...] = whole.reshape(toks, n_head, HD).astype(BF16)
+
     for part in (1, 0):
         def take(d):
             back_copy(part, d).wait()
@@ -541,12 +572,12 @@
         for d in sends:
             kv_copy(part, d).start()
         kv_out[head, part] = kv_sum[part, pl.ds(pl.multiple_of(head * toks, 32), toks), :]
-    own_dq.wait()
-    for d in range(1, n_head):
-        dq_copy(d).wait()
-    for part in range(2):
-        for d in range(1, n_head):
-            kv_copy(part, d).wait()
+        if part == 0:
+            own_dq.wait()
+            for d in range(1, n_head):
+                dq_copy(d).wait()
+            finish(1)
+            finish(0)
 
 
 def per_device(
@@ -566,21 +597,21 @@
     hbm = pl.BlockSpec(memory_space=pl.ANY)
     dma = pltpu.SemaphoreType.DMA
 
-    lse = jnp.transpose(logsumexp.reshape(toks, n_head, group), (1, 0, 2))
-    lse = lse.reshape(n_head, rows // 128, 1, 128)
-    kv = jnp.transpose(jnp.stack([key_states, value_states]), (2, 0, 1, 3))
-
     slots = n_seq * most
     step = BLK * group
-    query_grad, kv_all = pl.pallas_call(
+    return pl.pallas_call(
         functools.partial(fused, n_seq, n_head, most, blocks, pieces),
         out_shape=[
             jax.ShapeDtypeStruct((toks, heads, HD), BF16),
-            jax.ShapeDtypeStruct((n_head, 2, toks, HD), BF16),
+            jax.ShapeDtypeStruct((toks, n_head, HD), BF16),
+            jax.ShapeDtypeStruct((toks, n_head, HD), BF16),
         ],
-        in_specs=[smem, smem, hbm, hbm, hbm, vmem, vmem],
-        out_specs=[hbm, vmem],
+        in_specs=[smem, smem, hbm, hbm, hbm, vmem, vmem, vmem],
+        out_specs=[hbm, vmem, vmem],
         scratch_shapes=[
+            pltpu.VMEM((n_head, 2, toks, HD), BF16),
+            pltpu.VMEM((n_head, 2, toks, HD), BF16),
+            pltpu.VMEM((n_head, rows // 128, 1, 128), F32),
             pltpu.SMEM((slots,), jnp.int32),
             pltpu.SMEM((per_row,), jnp.int32),
             pltpu.SMEM((slots,), jnp.int32),
@@ -621,11 +652,10 @@
             collective_id=0, has_side_effects=True, vmem_limit_bytes=60 << 20
         ),
         name="fused",
-    )(random_owner.T, random_slot.T, queries, output_grad, outputs, kv, lse)
-
-    key_grad = jnp.transpose(kv_all[:, 0], (1, 0, 2))
-    value_grad = jnp.transpose(kv_all[:, 1], (1, 0, 2))
-    return query_grad, key_grad, value_grad
+    )(
+        random_owner.T, random_slot.T, queries, output_grad, outputs,
+        key_states, value_states, logsumexp.T,
+    )
 
 
 def solution(mesh):

time: 136 us -> 133 us (0.978)
  local copies, waits for them, and re-layouts: 7.47 us -> 4.97 us
    reshape x2 -> x0, local copies, waits for them, and re-layouts: 1.95 us -> none  [the longest x1 1.01 us: per_device(): lse = jnp.transpose(logsumexp.reshape(toks, n_head, group), (1, 0, 2))]
    unnamed x5 -> x7, local copies, waits for them, and re-layouts: 3.14 us -> 4.97 us
where the time goes in v3:
time: 133 us
  Pallas kernels  127 us (95%)
  local copies, waits for them, and re-layouts  4.97 us (4%)
    pallas_call x1, Pallas kernels, per_device(): pl.pallas_call(functools.partial(fused, n_seq, n_head, most, blocks, piec...  127 us
    unnamed x7, local copies, waits for them, and re-layouts  4.97 us

profile of v3, /device:TPU:11, one launch (start us, length us, event | category | flops | bytes accessed | tf_op | source)
XLA Modules:
  0.0 132.9 jit_solution(11135283572467598489)
XLA Ops:
  0.6 127.3 %fused.1 = (bf16[288,32,128]{2,1,0:T(8,128)(2,1)}, bf16[288,4,128]{2,1,0:T(4,128)(2,1)}, bf16[288,4,128]{2,1,0:T(4,128)(2,1)}) custom-call(s32[3,72]{1,0:T(4,128)} %bitcast.4, s32[3,72]{1,0:T(4,128)} %bitcast.5, bf16[288,32,128]{2,1,0:T(8,128)(2,1)} %q_in.1, bf16[288,32,128]{2,1,0:T(8,128)(2,1)} %g_in.1, bf16[288,32,128]{2,1,0:T(8,128)(2,1)} %o_in.1, ...), custom_call_target="tpu_custom_call" | custom-call | tf_op jit(solution)/shard_map/fused/pallas_call | solution.py:602
  127.9 0.0 copy-start.1
  127.9 0.0 copy-start
  127.9 3.5 %copy.14 = bf16[288,32,128]{2,1,0:T(8,128)(2,1)} copy(bf16[288,32,128]{2,1,0:T(8,128)(2,1)} %get-tuple-element.6) | data formatting | bytes 4718592
  131.5 0.0 copy-done.1
  131.5 0.7 copy.15
  132.2 0.0 copy-done
  132.2 0.7 copy.16
Async XLA Ops:
  127.9 3.6 %copy-start.1 = (bf16[288,4,128]{2,1,0:T(4,128)(2,1)S(1)}, bf16[288,4,128]{2,1,0:T(4,128)(2,1)}, u32[]{:S(2)}) copy-start(bf16[288,4,128]{2,1,0:T(4,128)(2,1)} %get-tuple-element.7) | copy-start | bytes 884740
  127.9 4.3 %copy-start = (bf16[288,4,128]{2,1,0:T(4,128)(2,1)S(1)}, bf16[288,4,128]{2,1,0:T(4,128)(2,1)}, u32[]{:S(2)}) copy-start(bf16[288,4,128]{2,1,0:T(4,128)(2,1)} %get-tuple-element.8) | copy-start | bytes 884740

commit v4 on v3

--- a/solution.py
+++ b/solution.py
@@ -16,6 +16,7 @@
 F32 = jnp.float32
 BF16 = jnp.bfloat16
 LOG2E = math.log2(math.e)
+LIFT = 8.0
 
 
 def greet(n_seq, n_head, seq, head):
@@ -423,7 +424,7 @@
         for j in range(RND):
             rpart[0, b * RND + j] = dk[j * BLK : (j + 1) * BLK].astype(BF16)
         total = dq_acc[b] + dot(found(0, b), score_grad, 0, 0)
-        dq_all[pl.ds(at, BLK)] = (total.T * scaling).astype(BF16).reshape(BLK, group, HD)
+        dq_all[pl.ds(at, BLK)] = (total.T * (scaling * LIFT)).astype(BF16).reshape(BLK, group, HD)
 
     last = pieces - 1
     early = sum(stage < last for stage, _ in plan)
@@ -483,14 +484,14 @@
         return remote(src, kv_out.at[head, part], es.at[part, d], er.at[part, d], head=peer)
 
     def part_copy():
-        return remote(gpart, gall.at[seq], ps.at[0], pr.at[seq], seq=0)
+        return remote(gpart, gall.at[seq], ps.at[0], pr.at[seq], seq=lax.rem(seq, 2))
 
     down_grad = remote(halo_part.at[0], halo.at[0], hs.at[0], hr.at[0], seq=down)
     up_grad = remote(halo_part.at[1], halo.at[1], hs.at[1], hr.at[1], seq=up)
     down_grad.start()
     up_grad.start()
 
-    @pl.when(seq > 0)
+    @pl.when(seq > 1)
     def _():
         part_copy().start()
 
@@ -532,13 +533,12 @@
     def _():
         for part in range(2):
             loop(1, n_seq, lambda d: glob_copy(part, d).wait_send())
-        gall[0] = gpart[...]
 
     def finish(part):
         for d in range(1, n_head):
             kv_copy(part, d).wait()
         whole = jnp.concatenate([kv_out[p, part] for p in range(n_head)], axis=1).astype(F32)
-        (dk_out, dv_out)[part][...] = whole.reshape(toks, n_head, HD).astype(BF16)
+        (dk_out, dv_out)[part][...] = (whole * LIFT).reshape(toks, n_head, HD).astype(BF16)
 
     for part in (1, 0):
         def take(d):
@@ -547,20 +547,26 @@
 
         loop(1, n_seq, take)
         if part:
+            passed = remote(gpart, gall.at[1], ps.at[0], pr.at[1], seq=0)
+
+            def add(d):
+                remote(gpart, gall.at[d], ps.at[0], pr.at[d], seq=0).wait_recv()
+                gacc[...] += gall[d].astype(F32)
+
+            @pl.when(seq == 1)
+            def _():
+                loop(1, n_seq // 2, lambda i: add(2 * i + 1))
+                gpart[...] = gacc[...].astype(BF16)
+                passed.start()
+                passed.wait_send()
+
             @pl.when(seq == 0)
             def _():
-                def arrive(d):
-                    remote(gpart, gall.at[d], ps.at[0], pr.at[d], seq=0).wait_recv()
-
-                loop(1, n_seq, arrive)
-
-                def add(d):
-                    gacc[...] += gall[d].astype(F32)
-
-                loop(1, n_seq, add)
+                loop(1, (n_seq + 1) // 2, lambda i: add(2 * i))
+                add(1)
                 acc[:, BLK : BLK + G * BLK, :] += gacc[...]
 
-            @pl.when(seq > 0)
+            @pl.when(seq > 1)
             def _():
                 part_copy().wait_send()
 
@@ -599,7 +605,7 @@
 
     slots = n_seq * most
     step = BLK * group
-    return pl.pallas_call(
+    grads = pl.pallas_call(
         functools.partial(fused, n_seq, n_head, most, blocks, pieces),
         out_shape=[
             jax.ShapeDtypeStruct((toks, heads, HD), BF16),
@@ -656,6 +662,7 @@
         random_owner.T, random_slot.T, queries, output_grad, outputs,
         key_states, value_states, logsumexp.T,
     )
+    return tuple(grad * jnp.asarray(1.0 / LIFT, BF16) for grad in grads)
 
 
 def solution(mesh):

time: 133 us -> 133 us (level)
  local copies, waits for them, and re-layouts: 4.97 us -> 0.01 us
  other arithmetic: 0 us -> 4.4 us
    unnamed x7 -> x4, local copies, waits for them, and re-layouts: 4.97 us -> 0.01 us
    mul x0 -> x2, other arithmetic: none -> 4.4 us  [per_device(): return tuple((grad * jnp.asarray(1.0 / LIFT, BF16) for grad in grads))]
where the time goes in v4:
time: 133 us; the launch traced here: 132 us
  Pallas kernels  127 us (95%)
  other arithmetic  4.4 us (3%)
    pallas_call x1, Pallas kernels, per_device(): pl.pallas_call(functools.partial(fused, n_seq, n_head, most, blocks, piec...  127 us
    mul x2, other arithmetic, per_device(): return tuple((grad * jnp.asarray(1.0 / LIFT, BF16) for grad in grads))  4.4 us

profile of v4, /device:TPU:11, one launch (start us, length us, event | category | flops | bytes accessed | tf_op | source)
XLA Modules:
  0.0 132.4 jit_solution(3522951357976861472)
XLA Ops:
  0.6 127.3 %fused.1 = (bf16[288,32,128]{2,1,0:T(8,128)(2,1)}, bf16[288,4,128]{2,1,0:T(4,128)(2,1)}, bf16[288,4,128]{2,1,0:T(4,128)(2,1)}) custom-call(s32[3,72]{1,0:T(4,128)} %bitcast.4, s32[3,72]{1,0:T(4,128)} %bitcast.5, bf16[288,32,128]{2,1,0:T(8,128)(2,1)} %q_in.1, bf16[288,32,128]{2,1,0:T(8,128)(2,1)} %g_in.1, bf16[288,32,128]{2,1,0:T(8,128)(2,1)} %o_in.1, ...), custom_call_target="tpu_custom_call" | custom-call | tf_op jit(solution)/shard_map/fused/pallas_call | solution.py:608
  127.9 0.0 copy-start
  128.0 0.0 copy-start.1
  128.0 3.3 %broadcast_multiply_fusion = bf16[288,32,128]{2,1,0:T(8,128)(2,1)} fusion(bf16[288,32,128]{2,1,0:T(8,128)(2,1)} %get-tuple-element.6), kind=kLoop, calls=%fused_computation | loop fusion | flops 1179648 | bytes 4718592 | tf_op jit(solution)/shard_map/mul | solution.py:665
  131.3 0.0 copy-done
  131.3 0.0 copy-done.1
  131.3 1.1 broadcast_multiply_fusion.1
Async XLA Ops:
  127.9 3.4 %copy-start = (bf16[288,4,128]{2,1,0:T(4,128)(2,1)S(1)}, bf16[288,4,128]{2,1,0:T(4,128)(2,1)}, u32[]{:S(2)}) copy-start(bf16[288,4,128]{2,1,0:T(4,128)(2,1)} %get-tuple-element.7) | copy-start | bytes 884740
  128.0 3.3 %copy-start.1 = (bf16[288,4,128]{2,1,0:T(4,128)(2,1)S(1)}, bf16[288,4,128]{2,1,0:T(4,128)(2,1)}, u32[]{:S(2)}) copy-start(bf16[288,4,128]{2,1,0:T(4,128)(2,1)} %get-tuple-element.8) | copy-start | bytes 884740
